TPU v7x, 32 devices: a whole 2x2x4 slice. The times are simulated.
32 devices in a mesh: chan: 16 (over z, y, core), band: 2 (over x).
Axes of the slice: x: 2, y: 2, z: 4, core: 2. Of those that a mesh axis runs over, the one named last changes fastest.
Arguments:
- strain: bfloat16 [4096, 4, 4096], P('chan', None, 'band'), may hold values from -6 to 6
- band_start: int32 [2], replicated, may hold values from 4 to 818
Outputs:
- coherency: bfloat16 [2, 2, 4096, 4096], P('band', None, 'chan')
All inputs are finite; a program needn't handle non-finite values.
Results may differ from a plain program's by a relative error of at most 0.0056.
Values may be sent and summed in bfloat16 or wider, within the bound.
A program may use at most 64 MiB of HBM per device.

v0:
```python
import math
import jax
import jax.numpy as jnp
from jax import lax
from jax.sharding import PartitionSpec as P

WINDOW_SAMPLES = 4096
K = 32


def dft_table(freqs, positions):
    phase_angles = positions[:, None, None] * freqs[None, :, :] % WINDOW_SAMPLES
    angles = phase_angles.astype(jnp.float32) * (2.0 * math.pi / WINDOW_SAMPLES)
    taper = 0.5 - 0.5 * jnp.cos(positions.astype(jnp.float32) * (2.0 * math.pi / WINDOW_SAMPLES))
    cosine = taper[:, None, None] * jnp.cos(angles)
    sine = -taper[:, None, None] * jnp.sin(angles)
    return jnp.concatenate([cosine, sine], axis=2).astype(jnp.bfloat16)


def whiten(spectrum, chans, windows):
    power = jnp.mean(spectrum * spectrum, axis=1, keepdims=True)
    whitened = (spectrum * lax.rsqrt(power + 1e-06)).astype(jnp.bfloat16)
    return (
        whitened.reshape(chans, windows, 2, K).transpose(0, 2, 1, 3).reshape(chans, 2 * windows * K)
    )


def cross_block(local_panel_rows, other_panel):
    half_feat = other_panel.shape[1] // 2
    rotated = jnp.concatenate([-other_panel[:, half_feat:], other_panel[:, :half_feat]], axis=1)
    stacked_spectra = jnp.stack([other_panel, rotated])
    cross_product = jnp.einsum(
        "gb,ozb->ogz", local_panel_rows, stacked_spectra, preferred_element_type=jnp.float32
    )
    return (cross_product * (1.0 / (2.0 * K))).astype(jnp.bfloat16)


def shards(strain, band_start):
    chans, windows, samp_dev = strain.shape
    flat = strain.reshape(chans * windows, samp_dev)
    band_index = lax.axis_index("band")
    bins = jnp.arange(K, dtype=jnp.int32)
    positions = band_index * samp_dev + jnp.arange(samp_dev, dtype=jnp.int32)
    own_rows = band_start.shape[0] // lax.axis_size("band")
    table = dft_table(band_start[:, None] + bins[None, :], positions)
    partial_sum = jnp.dot(
        flat,
        table.reshape(samp_dev, own_rows * lax.axis_size("band") * 2 * K),
        preferred_element_type=jnp.float32,
    )
    spectrum = lax.psum_scatter(
        partial_sum.reshape(chans * windows, own_rows * lax.axis_size("band"), 2 * K).transpose(
            1, 0, 2
        ),
        "band",
        scatter_dimension=0,
        tiled=True,
    )[0]
    panel = whiten(spectrum, chans, windows)
    result = cross_block(panel, lax.all_gather(panel, "chan", axis=0, tiled=True))
    return result[None]


def solution(mesh):
    return jax.shard_map(
        shards,
        mesh=mesh,
        in_specs=(P("chan", None, "band"), P()),
        out_specs=P("band", None, "chan", None),
        check_vma=False,
    )
```

profile of v0, /device:TPU:0, one launch (start us, length us, event | category | flops | bytes accessed | tf_op | source)
XLA Modules:
  0.0 110.6 jit_solution(17581041792112892675)
XLA Ops:
  6.5 0.0 reduce-scatter.2.cloned.1.call-start
  6.5 0.1 multiply_subtract_fusion
  6.6 0.7 iota_add_fusion.1
  7.3 6.9 %reshape.73 = bf16[1024,2048]{1,0:T(8,128)(2,1)} reshape(bf16[256,4,2048]{2,1,0:T(4,128)(2,1)} %param.2) | data formatting | bytes 8388608 | tf_op jit(solution)/shard_map/reshape | solution.py:40
  14.2 2.3 %multiply_convert_fusion.3 = (bf16[2048,2,32]{0,2,1:T(8,128)(2,1)S(1)}, bf16[2048,2,32]{0,2,1:T(8,128)(2,1)S(1)}) fusion(s32[2,32]{1,0:T(2,128)S(1)} %iota_add_fusion.1, s32[2048]{0:T(1024)S(1)} %iota_add_fusion, f32[2048]{0:T(1024)S(1)} %get-tuple-element.9, f32[2048]{0:T(1024)S(1)} %get-tuple-element.10), kind=kLoop, calls=%fused_computation.20 | loop fusion | flops 2359296 | bytes 549120 | tf_op jit(solution)/shard_map/convert
  16.5 3.7 %fusion.10 = f32[128,1024]{1,0:T(8,128)S(1)} fusion(bf16[2048,128]{0,1:T(8,128)(2,1)S(1)} %bitcast.22, bf16[1024,2048]{1,0:T(8,128)(2,1)} %reshape.73), kind=kOutput, calls=%fused_computation.27 | convolution fusion | flops 536870912 | bytes 5242880 | tf_op jit(solution)/shard_map/dot_general | solution.py:46
  20.2 1.3 %copy.5 = f32[1024,2,64]{2,0,1:T(8,128)} copy(f32[1024,2,64]{0,2,1:T(8,128)S(1)} %bitcast.21) | data formatting | bytes 1048576 | tf_op jit(solution)/shard_map/reshape | solution.py:52
  21.5 0.0 reduce-scatter.2.cloned.1.call-update
  21.6 0.0 all-gather.2.cloned.1.call-start
  21.6 23.2 %reduce-scatter.2.cloned.1.call-done = f32[1,1024,64]{2,1,0:T(8,128)} async-done(((f32[2,1024,64]{2,1,0:T(8,128)}), f32[1,1024,64]{2,1,0:T(8,128)}) %reduce-scatter.2.cloned.1.call-update) | async-done | bytes 262160 | tf_op jit(solution)/shard_map/reduce_scatter | solution.py:51
  44.8 1.2 %multiply_reduce_fusion = f32[1024]{0:T(1024)S(1)} fusion(f32[1,1024,64]{2,1,0:T(8,128)} %reduce-scatter.2.cloned.1.call-done), kind=kLoop, calls=%fused_computation.18 | loop fusion | flops 130048 | bytes 266240 | tf_op jit(solution)/shard_map/reduce_sum | solution.py:21
  46.1 0.1 rsqrt.12
  46.2 1.7 %squeeze.3 = f32[256,4,2,32]{3,2,1,0:T(2,128)S(1)} reshape(f32[1,1024,64]{2,1,0:T(8,128)} %reduce-scatter.2.cloned.1.call-done) | data formatting | bytes 524288 | tf_op jit(solution)/shard_map/squeeze | solution.py:51
  47.9 1.7 %fusion.7 = bf16[256,2,4,32]{3,1,2,0:T(2,128)(2,1)S(1)} fusion(f32[256,4,2,32]{3,2,1,0:T(2,128)S(1)} %squeeze.3, f32[256,4]{1,0:T(8,128)S(1)} %rsqrt.12), kind=kLoop, calls=%fused_computation.16 | loop fusion | flops 131072 | bytes 397312 | tf_op jit(solution)/shard_map/transpose | solution.py:24
  49.6 0.5 copy.6
  50.1 0.8 copy.7
  50.8 0.0 all-gather.2.cloned.1.call-update
  50.9 41.6 %all-gather.2.cloned.1.call-done = bf16[4096,256]{1,0:T(8,128)(2,1)} async-done(((bf16[256,256]{1,0:T(8,128)(2,1)}), bf16[4096,256]{1,0:T(8,128)(2,1)}) %all-gather.2.cloned.1.call-update) | async-done | bytes 2097168 | tf_op jit(solution)/shard_map/all_gather | solution.py:60
  92.5 0.0 copy-start
  92.5 1.9 %slice_negate_fusion = (bf16[4096,128]{1,0:T(8,128)(2,1)S(1)}, bf16[4096,128]{1,0:T(8,128)(2,1)S(1)}) fusion(bf16[4096,256]{1,0:T(8,128)(2,1)} %all-gather.2.cloned.1.call-done), kind=kLoop, calls=%fused_computation.6 | loop fusion | flops 524288 | bytes 4194304 | tf_op jit(solution)/shard_map/neg | solution.py:30
  94.4 0.2 maximum_bitcast_fusion
  94.6 0.1 copy-done
  94.7 2.7 %fusion = bf16[1,2,256,4096]{2,3,1,0:T(8,128)(2,1)} fusion(bf16[256,256,1]{0,1,2:T(8,128)(2,1)S(1)} %bitcast.25, bf16[1,4096,256]{2,1,0:T(8,128)(2,1)S(1)} %maximum_bitcast_fusion, bf16[1,4096,256]{2,1,0:T(8,128)(2,1)S(1)} %bitcast.23), kind=kOutput, calls=%fused_computation.1 | convolution fusion | flops 1080033280 | bytes 8519680 | tf_op jit(solution)/shard_map/gb,ozb->ogz/dot_general | solution.py:32
  97.4 6.3 %copy.9 = bf16[1,2,256,4096]{3,2,1,0:T(8,128)(2,1)} copy(bf16[1,2,256,4096]{2,3,1,0:T(8,128)(2,1)} %fusion) | data formatting | bytes 8388608 | tf_op jit(solution)/shard_map/broadcast_in_dim | solution.py:61
  (3 shorter events, 0.0 us)
Async XLA Ops:
  6.5 38.3 %reduce-scatter.2.cloned.1.call-start = ((), (), s32[]{:S(2)}) async-start(), calls=%async_computation.1 | async-start | bytes 1572864 | tf_op jit(solution)/shard_map/reduce_scatter | solution.py:51
  21.6 70.9 %all-gather.2.cloned.1.call-start = ((), (), s32[]{:S(2)}) async-start(), calls=%async_computation.2 | async-start | bytes 2228224 | tf_op jit(solution)/shard_map/all_gather | solution.py:60
  92.5 2.2 %copy-start = (bf16[4096,256]{1,0:T(8,128)(2,1)S(1)}, bf16[4096,256]{1,0:T(8,128)(2,1)}, u32[]{:S(2)}) copy-start(bf16[4096,256]{1,0:T(8,128)(2,1)} %all-gather.2.cloned.1.call-done) | copy-start | bytes 6291460
Sparse Core Ops, SparseCore 0:
  21.7 23.0 reduce-scatter.1
  51.0 41.4 all-gather.1
where the time goes:
time: 111 us
  waiting for transfers between devices  64.9 us (58%)
  local copies, waits for them, and re-layouts  17.6 us (16%)
  between operations  13.5 us (12%)
  other arithmetic  8.16 us (7%)
  matrix products  6.46 us (6%)
    all_gather x1, waiting for transfers between devices, shards(): lax.all_gather(panel, 'chan', axis=0, tiled=True)  41.6 us
    reduce_scatter x1, waiting for transfers between devices, shards(): lax.psum_scatter(partial_sum.reshape(chans * windows, own_rows * lax.axis...  23.2 us
    reshape x1, local copies, waits for them, and re-layouts, shards(): flat = strain.reshape(chans * windows, samp_dev)  6.86 us
    broadcast_in_dim x1, local copies, waits for them, and re-layouts, shards(): return result[None]  6.31 us
    dot_general x1, matrix products, shards(): jnp.dot(flat, table.reshape(samp_dev, own_rows * lax.axis_size('band') *...  3.73 us
    dot_general x1, matrix products, cross_block(): jnp.einsum('gb,ozb->ogz', local_panel_rows, stacked_spectra, preferred_el...  2.73 us
    another operation x1, other arithmetic  2.25 us
  transfers between devices with their start and end apart: 2, of which 2 were waited for; matrix products, arithmetic and copies ran while one was open for 0% of the time, Pallas kernels for 0%

commit v1 on v0

--- a/solution.py
+++ b/solution.py
@@ -6,6 +6,28 @@
 
 WINDOW_SAMPLES = 4096
 K = 32
+
+
+def in_order(pieces, dim):
+    dims = list(pieces.shape[1:])
+    dims[dim] *= pieces.shape[0]
+    return jnp.moveaxis(pieces, 0, dim).reshape(dims)
+
+
+def grow_blocks(value, axis):
+    length = lax.axis_size(axis)
+    pieces = value[None]
+    for level in range(length.bit_length() - 1):
+        apart = 1 << level
+        theirs = lax.ppermute(pieces, axis, [(i, i ^ apart) for i in range(length)])
+        both = jnp.stack([pieces, theirs])
+        upper = lax.axis_index(axis) >> level & 1
+        pieces = jnp.where(upper == 0, both, both[::-1]).reshape(-1, *value.shape)
+    return pieces
+
+
+def doubled_up(x, axis, dim):
+    return in_order(grow_blocks(x, axis), dim)
 
 
 def dft_table(freqs, positions):
@@ -57,7 +79,7 @@
         tiled=True,
     )[0]
     panel = whiten(spectrum, chans, windows)
-    result = cross_block(panel, lax.all_gather(panel, "chan", axis=0, tiled=True))
+    result = cross_block(panel, doubled_up(panel, "chan", 0))
     return result[None]
 
 

time: 111 us -> 139 us (1.25)
  waiting for transfers between devices: 64.9 us -> 87.5 us
  starting transfers between devices: 0.04 us -> 5.68 us
    ppermute x0 -> x4, waiting for transfers between devices: none -> 64.3 us  [grow_blocks(): theirs = lax.ppermute(pieces, axis, [(i, i ^ apart) for i in range(length)])]
    all_gather x1 -> x0, waiting for transfers between devices: 41.6 us -> none  [shards(): lax.all_gather(panel, 'chan', axis=0, tiled=True)]
    ppermute x0 -> x4, starting transfers between devices: none -> 5.68 us  [grow_blocks(): theirs = lax.ppermute(pieces, axis, [(i, i ^ apart) for i in range(length)])]
    neg x1, other arithmetic: 1.89 us -> 0.25 us  [cross_block(): -other_panel[:, half_feat:]]
  transfers between devices with their start and end apart: 2 -> 5, of which waited for: 2 -> 5; matrix products, arithmetic and copies ran while one was open for 0% -> 0% of each run, Pallas kernels for 0% -> 0%
where the time goes in v1:
time: 139 us; the launch traced here: 138 us
  waiting for transfers between devices  87.5 us (63%)
  local copies, waits for them, and re-layouts  17.3 us (12%)
  between operations  13.5 us (10%)
  other arithmetic  7.71 us (6%)
  matrix products  6.48 us (5%)
  starting transfers between devices  5.68 us (4%)
    ppermute x4, waiting for transfers between devices, grow_blocks(): theirs = lax.ppermute(pieces, axis, [(i, i ^ apart) for i in range(length)])  64.3 us
    reduce_scatter x1, waiting for transfers between devices, shards(): lax.psum_scatter(partial_sum.reshape(chans * windows, own_rows * lax.axis...  23.3 us
    reshape x1, local copies, waits for them, and re-layouts, shards(): flat = strain.reshape(chans * windows, samp_dev)  6.86 us
    broadcast_in_dim x1, local copies, waits for them, and re-layouts, shards(): return result[None]  6.31 us
    ppermute x4, starting transfers between devices, grow_blocks(): theirs = lax.ppermute(pieces, axis, [(i, i ^ apart) for i in range(length)])  5.68 us
    dot_general x1, matrix products, shards(): jnp.dot(flat, table.reshape(samp_dev, own_rows * lax.axis_size('band') *...  3.73 us
  transfers between devices with their start and end apart: 5, of which 5 were waited for; matrix products, arithmetic and copies ran while one was open for 0% of the time, Pallas kernels for 0%

profile of v1, /device:TPU:0, one launch (start us, length us, event | category | flops | bytes accessed | tf_op | source)
XLA Modules:
  0.0 138.2 jit_solution(6035726031560936635)
XLA Ops:
  6.5 0.0 reduce-scatter.2.cloned.1.call-start
  6.5 0.1 multiply_subtract_fusion
  6.6 0.7 iota_add_fusion.1
  7.3 6.9 %reshape.82 = bf16[1024,2048]{1,0:T(8,128)(2,1)} reshape(bf16[256,4,2048]{2,1,0:T(4,128)(2,1)} %param.2) | data formatting | bytes 8388608 | tf_op jit(solution)/shard_map/reshape | solution.py:62
  14.2 2.3 %multiply_convert_fusion.3 = (bf16[2048,2,32]{0,2,1:T(8,128)(2,1)S(1)}, bf16[2048,2,32]{0,2,1:T(8,128)(2,1)S(1)}) fusion(s32[2,32]{1,0:T(2,128)S(1)} %iota_add_fusion.1, s32[2048]{0:T(1024)S(1)} %iota_add_fusion, f32[2048]{0:T(1024)S(1)} %get-tuple-element.11, f32[2048]{0:T(1024)S(1)} %get-tuple-element.12), kind=kLoop, calls=%fused_computation.26 | loop fusion | flops 2359296 | bytes 549120 | tf_op jit(solution)/shard_map/convert
  16.5 3.7 %fusion.12 = f32[128,1024]{1,0:T(8,128)S(1)} fusion(bf16[2048,128]{0,1:T(8,128)(2,1)S(1)} %bitcast.41, bf16[1024,2048]{1,0:T(8,128)(2,1)} %reshape.82), kind=kOutput, calls=%fused_computation.37 | convolution fusion | flops 536870912 | bytes 5242880 | tf_op jit(solution)/shard_map/dot_general | solution.py:68
  20.2 1.3 copy.5
  21.5 0.0 reduce-scatter.2.cloned.1.call-update
  21.6 23.3 %reduce-scatter.2.cloned.1.call-done = f32[1,1024,64]{2,1,0:T(8,128)} async-done(((f32[2,1024,64]{2,1,0:T(8,128)}), f32[1,1024,64]{2,1,0:T(8,128)}) %reduce-scatter.2.cloned.1.call-update) | async-done | bytes 262160 | tf_op jit(solution)/shard_map/reduce_scatter | solution.py:73
  44.8 1.2 multiply_reduce_fusion
  46.1 0.1 rsqrt.12
  46.2 1.7 %squeeze.3 = f32[256,4,2,32]{3,2,1,0:T(2,128)S(1)} reshape(f32[1,1024,64]{2,1,0:T(8,128)} %reduce-scatter.2.cloned.1.call-done) | data formatting | bytes 524288 | tf_op jit(solution)/shard_map/squeeze | solution.py:73
  47.9 1.7 %fusion.7 = bf16[256,2,4,32]{3,1,2,0:T(2,128)(2,1)S(1)} fusion(f32[256,4,2,32]{3,2,1,0:T(2,128)S(1)} %squeeze.3, f32[256,4]{1,0:T(8,128)S(1)} %rsqrt.12), kind=kLoop, calls=%fused_computation.21 | loop fusion | flops 131072 | bytes 397312 | tf_op jit(solution)/shard_map/transpose | solution.py:46
  49.6 0.5 copy.6
  50.1 0.1 collective-permute-start
  50.2 1.3 collective-permute-done
  51.5 0.1 fusion.9
  51.6 1.6 %collective-permute-start.1 = (bf16[2,256,256]{1,2,0:T(8,128)(2,1)S(1)}, bf16[2,256,256]{1,2,0:T(8,128)(2,1)S(1)}, u32[]{:S(2)}, u32[]{:S(2)}) collective-permute-start(bf16[2,256,256]{1,2,0:T(8,128)(2,1)S(1)} %get-tuple-element.8), channel_id=1, source_target_pairs={{0,4},{2,6},{4,0},{6,2},{8,12},{10,14},{12,8},{14,10},{16,20},{18,... | collective-permute-start | bytes 786440 | tf_op jit(solution)/shard_map/ppermute | solution.py:22
  53.2 6.9 %collective-permute-done.1 = bf16[2,256,256]{1,2,0:T(8,128)(2,1)S(1)} collective-permute-done((bf16[2,256,256]{1,2,0:T(8,128)(2,1)S(1)}, bf16[2,256,256]{1,2,0:T(8,128)(2,1)S(1)}, u32[]{:S(2)}, u32[]{:S(2)}) %collective-permute-start.1) | collective-permute-done | bytes 262176 | tf_op jit(solution)/shard_map/ppermute | solution.py:22
  60.0 0.1 pad_maximum_fusion.3
  60.1 0.1 reverse_select_fusion.2
  60.2 1.6 %collective-permute-start.2 = (bf16[4,256,256]{1,2,0:T(8,128)(2,1)S(1)}, bf16[4,256,256]{1,2,0:T(8,128)(2,1)S(1)}, u32[]{:S(2)}, u32[]{:S(2)}) collective-permute-start(bf16[4,256,256]{1,2,0:T(8,128)(2,1)S(1)} %bitcast.42), channel_id=1, source_target_pairs={{0,8},{2,10},{4,12},{6,14},{8,0},{10,2},{12,4},{14,6},{16,24},{18,... | collective-permute-start | bytes 1572872 | tf_op jit(solution)/shard_map/ppermute | solution.py:22
  61.8 11.6 %collective-permute-done.2 = bf16[4,256,256]{1,2,0:T(8,128)(2,1)S(1)} collective-permute-done((bf16[4,256,256]{1,2,0:T(8,128)(2,1)S(1)}, bf16[4,256,256]{1,2,0:T(8,128)(2,1)S(1)}, u32[]{:S(2)}, u32[]{:S(2)}) %collective-permute-start.2) | collective-permute-done | bytes 524320 | tf_op jit(solution)/shard_map/ppermute | solution.py:22
  73.4 0.1 pad_maximum_fusion.1
  73.5 0.2 reverse_select_fusion.1
  73.7 0.5 copy.8
  74.2 2.5 %collective-permute-start.3 = (bf16[8,256,256]{2,1,0:T(8,128)(2,1)S(1)}, bf16[8,256,256]{2,1,0:T(8,128)(2,1)S(1)}, u32[]{:S(2)}, u32[]{:S(2)}) collective-permute-start(bf16[8,256,256]{2,1,0:T(8,128)(2,1)S(1)} %bitcast.38), channel_id=1, source_target_pairs={{0,16},{2,18},{4,20},{6,22},{8,24},{10,26},{12,28},{14,30},{16,0},... | collective-permute-start | bytes 3145736 | tf_op jit(solution)/shard_map/ppermute | solution.py:22
  76.7 44.5 %collective-permute-done.3 = bf16[8,256,256]{2,1,0:T(8,128)(2,1)S(1)} collective-permute-done((bf16[8,256,256]{2,1,0:T(8,128)(2,1)S(1)}, bf16[8,256,256]{2,1,0:T(8,128)(2,1)S(1)}, u32[]{:S(2)}, u32[]{:S(2)}) %collective-permute-start.3) | collective-permute-done | bytes 1048608 | tf_op jit(solution)/shard_map/ppermute | solution.py:22
  121.1 0.2 pad_maximum_fusion
  121.3 0.5 reverse_select_fusion
  121.8 0.2 slice_negate_fusion
  122.1 0.2 maximum_bitcast_fusion
  122.3 2.7 %fusion = bf16[1,2,256,4096]{2,3,1,0:T(8,128)(2,1)} fusion(bf16[256,256,1]{0,1,2:T(8,128)(2,1)S(1)} %bitcast.47, bf16[1,4096,256]{2,1,0:T(8,128)(2,1)S(1)} %maximum_bitcast_fusion, bf16[1,4096,256]{2,1,0:T(8,128)(2,1)S(1)} %bitcast.36), kind=kOutput, calls=%fused_computation.1 | convolution fusion | flops 1080033280 | bytes 8519680 | tf_op jit(solution)/shard_map/gb,ozb->ogz/dot_general | solution.py:54
  125.0 6.3 %copy.12 = bf16[1,2,256,4096]{3,2,1,0:T(8,128)(2,1)} copy(bf16[1,2,256,4096]{2,3,1,0:T(8,128)(2,1)} %fusion) | data formatting | bytes 8388608 | tf_op jit(solution)/shard_map/broadcast_in_dim | solution.py:83
  (4 shorter events, 0.1 us)
Async XLA Ops:
  6.5 38.3 %reduce-scatter.2.cloned.1.call-start = ((), (), s32[]{:S(2)}) async-start(), calls=%async_computation.1 | async-start | bytes 1572864 | tf_op jit(solution)/shard_map/reduce_scatter | solution.py:73
  50.1 1.4 %collective-permute-start = (bf16[1,256,256]{1,2,0:T(8,128)(2,1)S(1)}, bf16[1,256,256]{1,2,0:T(8,128)(2,1)S(1)}, u32[]{:S(2)}, u32[]{:S(2)}) collective-permute-start(bf16[1,256,256]{1,2,0:T(8,128)(2,1)S(1)} %bitcast.45), channel_id=1, source_target_pairs={{0,2},{2,0},{4,6},{6,4},{8,10},{10,8},{12,14},{14,12},{16,18},{18,... | collective-permute-start | bytes 393224 | tf_op jit(solution)/shard_map/ppermute | solution.py:22
  51.6 8.4 %collective-permute-start.1 = (bf16[2,256,256]{1,2,0:T(8,128)(2,1)S(1)}, bf16[2,256,256]{1,2,0:T(8,128)(2,1)S(1)}, u32[]{:S(2)}, u32[]{:S(2)}) collective-permute-start(bf16[2,256,256]{1,2,0:T(8,128)(2,1)S(1)} %get-tuple-element.8), channel_id=1, source_target_pairs={{0,4},{2,6},{4,0},{6,2},{8,12},{10,14},{12,8},{14,10},{16,20},{18,... | collective-permute-start | bytes 786440 | tf_op jit(solution)/shard_map/ppermute | solution.py:22
  60.2 13.2 %collective-permute-start.2 = (bf16[4,256,256]{1,2,0:T(8,128)(2,1)S(1)}, bf16[4,256,256]{1,2,0:T(8,128)(2,1)S(1)}, u32[]{:S(2)}, u32[]{:S(2)}) collective-permute-start(bf16[4,256,256]{1,2,0:T(8,128)(2,1)S(1)} %bitcast.42), channel_id=1, source_target_pairs={{0,8},{2,10},{4,12},{6,14},{8,0},{10,2},{12,4},{14,6},{16,24},{18,... | collective-permute-start | bytes 1572872 | tf_op jit(solution)/shard_map/ppermute | solution.py:22
  74.2 46.9 %collective-permute-start.3 = (bf16[8,256,256]{2,1,0:T(8,128)(2,1)S(1)}, bf16[8,256,256]{2,1,0:T(8,128)(2,1)S(1)}, u32[]{:S(2)}, u32[]{:S(2)}) collective-permute-start(bf16[8,256,256]{2,1,0:T(8,128)(2,1)S(1)} %bitcast.38), channel_id=1, source_target_pairs={{0,16},{2,18},{4,20},{6,22},{8,24},{10,26},{12,28},{14,30},{16,0},... | collective-permute-start | bytes 3145736 | tf_op jit(solution)/shard_map/ppermute | solution.py:22
Sparse Core Ops, SparseCore 0:
  21.7 23.0 reduce-scatter.1
